TPU v7x, 256 devices: a whole 4x4x8 slice. The times are simulated.
256 devices in a mesh: cols: 128 (over x, y, z), rows: 2 (over core).
Axes of the slice: x: 4, y: 4, z: 8, core: 2. Of those that a mesh axis runs over, the one named last changes fastest.
Arguments:
- activations: bfloat16 [256, 65536], P('rows', 'cols'), may hold values from 0 to 16
- weights: bfloat16 [2, 512, 40, 128, 128], P(None, 'cols', 'rows'), may hold values from -0.15625 to 0.15625
- biases: float32 [2, 65536], P(None, 'cols'), may hold values from -6 to 2
- pattern: int32 [2, 512, 40], P(None, 'cols'), may hold values from 0 to 511, as said below
- counts: int32 [2, 512], P(None, 'cols'), may hold values from 1 to 40, 10240 in all within a row
Outputs:
- result: bfloat16 [256, 65536], P('rows', 'cols')
Inputs may be any that keep to these rules, and one draw needn't show every extreme that they name: `pattern`: the 40 entries of a column block are distinct. All entries of the 4 column blocks held by one index of cols, live or not, name at most 1 different blocks among the 4 blocks held by any one index of cols, and exactly 1 for some. In each layer the counts sum to 10240.
All inputs are finite; a program needn't handle non-finite values. No bound on the sum of `counts` on one device may be relied on, other than what follows from the above.
Results may differ from a plain program's by a relative error of at most 0.0047.
Values may be sent and summed in bfloat16 or wider, within the bound.
A program may use at most 128 MiB of HBM per device.

v0:
```python
import jax
import jax.numpy as jnp
from jax import lax
from jax.sharding import PartitionSpec as P


def per_device(activations, weights, biases, pattern, counts):
    rows_here = activations.shape[0]
    owned = pattern.shape[1]
    slot_count = pattern.shape[2]
    block_size = weights.shape[-1]
    layers = weights.shape[0]
    devices = lax.axis_size("cols")
    nblocks_all = owned * devices
    current = activations
    for layer in range(layers):
        weight_all = lax.all_gather(weights[layer], "rows", axis=1, tiled=True)
        live_slots = (jnp.arange(slot_count)[None, :] < counts[layer][:, None]).astype(jnp.bfloat16)
        weight_used = weight_all * live_slots[:, :, None, None]
        layer_bias = biases[layer]
        gathered = lax.all_gather(current, "cols", axis=1, tiled=True)
        all_blocks = gathered.reshape(rows_here, nblocks_all, block_size)
        selected = jnp.take(all_blocks, pattern[layer].reshape(-1), axis=1)
        items = selected.shape[0]
        picked = selected.reshape(items, owned, slot_count, block_size)
        total = jnp.einsum(
            "sjkb,jkbc->sjc", picked, weight_used, preferred_element_type=jnp.float32
        )
        shifted = total.reshape(items, owned * block_size) + layer_bias[None, :]
        current = jnp.clip(shifted, 0.0, 32.0).astype(jnp.bfloat16)
    return current


def solution(mesh):
    return jax.shard_map(
        per_device,
        mesh=mesh,
        in_specs=(
            P("rows", "cols"),
            P(None, "cols", "rows", None, None),
            P(None, "cols"),
            P(None, "cols", None),
            P(None, "cols"),
        ),
        out_specs=P("rows", "cols"),
        check_vma=False,
    )
```

profile of v0, /device:TPU:8, one launch (start us, length us, event | category | flops | bytes accessed | tf_op | source)
XLA Modules:
  0.0 414.9 jit_solution(2486084904053249132)
XLA Ops:
  6.5 0.0 all-gather.7.cloned.1.call-start
  6.5 1.7 copy.16
  8.2 0.0 all-gather.7.cloned.1.call-update
  8.2 0.0 copy-start
  8.2 0.0 copy-start.2
  8.2 0.0 copy-start.1
  8.3 0.0 all-gather.13.cloned.1.call-start
  8.3 7.0 %fusion.10 = (bf16[1,4,20,128,128]{4,3,2,1,0:T(8,128)(2,1)}, bf16[1,4,20,128,128]{4,3,2,1,0:T(8,128)(2,1)}) fusion(bf16[2,4,20,128,128]{4,3,2,1,0:T(8,128)(2,1)} %param.8), kind=kLoop, calls=%fused_computation.28 | loop fusion | bytes 10485760 | tf_op jit(solution)/shard_map/slice | solution.py:17
  15.3 0.0 all-gather.13.cloned.1.call-update
  15.3 0.0 all-gather.9.cloned.1.call-start
  15.4 0.0 copy-done
  15.4 0.1 reshape_squeeze.6
  15.5 0.1 fusion.9
  15.6 0.0 copy-done.1
  15.6 148.4 %all-gather.7.cloned.1.call-done = bf16[128,65536]{0,1:T(8,128)(2,1)} async-done(((bf16[128,512]{0,1:T(8,128)(2,1)}), bf16[128,65536]{0,1:T(8,128)(2,1)}) %all-gather.7.cloned.1.call-update) | async-done | bytes 16777232 | tf_op jit(solution)/shard_map/all_gather | solution.py:21
  164.0 22.7 %copy.17 = bf16[128,512,128]{2,0,1:T(8,128)(2,1)} copy(bf16[128,512,128]{0,2,1:T(8,128)(2,1)} %bitcast.44) | data formatting | bytes 33554432 | tf_op jit(solution)/shard_map/reshape | solution.py:22
  186.7 13.5 %gather_fusion = bf16[160,128,128]{2,1,0:T(8,128)(2,1)} fusion(bf16[128,512,128]{2,0,1:T(8,128)(2,1)} %copy.17, s32[1024]{0:T(1024)S(1)} %pad_clamp_fusion.1), kind=kCustom, calls=%fused_computation.clone | custom fusion | bytes 10486400 | tf_op jit(solution)/shard_map/jit(_take)/gather | solution.py:23
  200.1 5.3 %broadcast_select_fusion.1 = bf16[160,128,128]{2,1,0:T(8,128)(2,1)} fusion(bf16[160,128,128]{2,1,0:T(8,128)(2,1)} %gather_fusion, pred[160]{0:T(512)(128)(4,1)S(1)} %compare_and_fusion.1), kind=kLoop, calls=%fused_computation.7 | loop fusion | flops 2621440 | bytes 10485920 | tf_op jit(solution)/shard_map/jit(_take)/select_n | solution.py:23
  205.5 6.1 %fusion = f32[4,128,128,1]{2,1,3,0:T(8,128)S(1)} fusion(bf16[128,4,40,128]{3,0,2,1:T(8,128)(2,1)} %bitcast.46, bf16[1,4,40,128,128]{4,3,2,1,0:T(8,128)(2,1)} %all-gather.13.cloned.1.call-done, bf16[4,40]{1,0:T(4,128)(2,1)S(1)} %fusion.9), kind=kOutput, calls=%fused_computation.3 | convolution fusion | flops 673710080 | bytes 10748224 | tf_op jit(solution)/shard_map/sjkb,jkbc->sjc/dot_general | solution.py:26
  211.6 0.8 fusion.7
  212.4 0.0 all-gather.9.cloned.1.call-update
  212.4 0.2 all-gather.11.cloned.1.call-start
  212.6 0.3 all-gather.11.cloned.1.call-update
  213.0 0.1 reshape_squeeze.7
  213.1 0.1 fusion.8
  213.2 146.7 %all-gather.9.cloned.1.call-done = bf16[128,65536]{0,1:T(8,128)(2,1)} async-done(((bf16[128,512]{0,1:T(8,128)(2,1)}), bf16[128,65536]{0,1:T(8,128)(2,1)}) %all-gather.9.cloned.1.call-update) | async-done | bytes 16777232 | tf_op jit(solution)/shard_map/all_gather | solution.py:21
  359.9 22.7 %copy.19 = bf16[128,512,128]{2,0,1:T(8,128)(2,1)} copy(bf16[128,512,128]{0,2,1:T(8,128)(2,1)} %bitcast.45) | data formatting | bytes 33554432 | tf_op jit(solution)/shard_map/reshape | solution.py:22
  382.6 13.5 %gather_fusion.1 = bf16[160,128,128]{2,1,0:T(8,128)(2,1)} fusion(bf16[128,512,128]{2,0,1:T(8,128)(2,1)} %copy.19, s32[1024]{0:T(1024)S(1)} %pad_clamp_fusion), kind=kCustom, calls=%fused_computation.1.clone | custom fusion | bytes 10486400 | tf_op jit(solution)/shard_map/jit(_take)/gather | solution.py:23
  396.0 5.3 %broadcast_select_fusion = bf16[160,128,128]{2,1,0:T(8,128)(2,1)} fusion(bf16[160,128,128]{2,1,0:T(8,128)(2,1)} %gather_fusion.1, pred[160]{0:T(512)(128)(4,1)S(1)} %compare_and_fusion), kind=kLoop, calls=%fused_computation.6 | loop fusion | flops 2621440 | bytes 10485920 | tf_op jit(solution)/shard_map/jit(_take)/select_n | solution.py:23
  401.4 6.1 %fusion.1 = f32[4,128,128,1]{2,1,3,0:T(8,128)S(1)} fusion(bf16[128,4,40,128]{3,0,2,1:T(8,128)(2,1)} %bitcast.47, bf16[1,4,40,128,128]{4,3,2,1,0:T(8,128)(2,1)} %all-gather.11.cloned.1.call-done, bf16[4,40]{1,0:T(4,128)(2,1)S(1)} %fusion.8), kind=kOutput, calls=%fused_computation.5 | convolution fusion | flops 673710080 | bytes 10748224 | tf_op jit(solution)/shard_map/sjkb,jkbc->sjc/dot_general | solution.py:26
  407.5 0.1 fusion.5
  407.6 0.8 copy.21
  (12 shorter events, 0.1 us)
Async XLA Ops:
  6.5 157.5 %all-gather.7.cloned.1.call-start = ((), (), s32[]{:S(2)}) async-start(), calls=%async_computation | async-start | bytes 16908288 | tf_op jit(solution)/shard_map/all_gather | solution.py:21
  8.2 7.2 %copy-start = (s32[2,4,40]{2,1,0:T(4,128)S(1)}, s32[2,4,40]{2,1,0:T(4,128)}, u32[]{:S(2)}) copy-start(s32[2,4,40]{2,1,0:T(4,128)} %param.10) | copy-start | bytes 3844
  8.2 7.3 %copy-start.2 = (s32[2,4]{1,0:T(2,128)S(1)}, s32[2,4]{1,0:T(2,128)}, u32[]{:S(2)}) copy-start(s32[2,4]{1,0:T(2,128)} %param.11) | copy-start | bytes 100
  8.2 7.4 %copy-start.1 = (f32[2,512]{1,0:T(2,128)S(1)}, f32[2,512]{1,0:T(2,128)}, u32[]{:S(2)}) copy-start(f32[2,512]{1,0:T(2,128)} %param.9) | copy-start | bytes 12292
  8.3 197.2 %all-gather.13.cloned.1.call-start = ((), (), s32[]{:S(2)}) async-start(), calls=%async_computation.3 | async-start | bytes 7864320 | tf_op jit(solution)/shard_map/all_gather | solution.py:17
  15.3 344.6 %all-gather.9.cloned.1.call-start = ((), (), s32[]{:S(2)}) async-start(), calls=%async_computation.1 | async-start | bytes 16908288 | tf_op jit(solution)/shard_map/all_gather | solution.py:21
  212.4 189.0 %all-gather.11.cloned.1.call-start = ((), (), s32[]{:S(2)}) async-start(), calls=%async_computation.2 | async-start | bytes 7864320 | tf_op jit(solution)/shard_map/all_gather | solution.py:17
Sparse Core Ops, SparseCore 0:
  11.0 152.9 all-gather.6
  165.8 17.6 all-gather.12
  212.5 147.3 all-gather.8
  361.6 17.6 all-gather.10
where the time goes:
time: 416 us; the launch traced here: 415 us
  waiting for transfers between devices  296 us (71%)
  local copies, waits for them, and re-layouts  81.9 us (20%)
  between operations  13.2 us (3%)
  matrix products  12.2 us (3%)
  other arithmetic  11.8 us (3%)
    all_gather x2, waiting for transfers between devices, per_device(): gathered = lax.all_gather(current, 'cols', axis=1, tiled=True)  295 us
    reshape x2, local copies, waits for them, and re-layouts, per_device(): all_blocks = gathered.reshape(rows_here, nblocks_all, block_size)  45.3 us
    gather x2, local copies, waits for them, and re-layouts, per_device(): selected = jnp.take(all_blocks, pattern[layer].reshape(-1), axis=1)  26.9 us
    dot_general x2, matrix products, per_device(): jnp.einsum('sjkb,jkbc->sjc', picked, weight_used, preferred_element_type=...  12.2 us
    select_n x4, other arithmetic, per_device(): selected = jnp.take(all_blocks, pattern[layer].reshape(-1), axis=1)  10.7 us
  transfers between devices with their start and end apart: 4, of which 2 were waited for; matrix products, arithmetic and copies ran while one was open for 22% of the time, Pallas kernels for 0%

commit v1 on v0

--- a/solution.py
+++ b/solution.py
@@ -18,7 +18,9 @@
         live_slots = (jnp.arange(slot_count)[None, :] < counts[layer][:, None]).astype(jnp.bfloat16)
         weight_used = weight_all * live_slots[:, :, None, None]
         layer_bias = biases[layer]
-        gathered = lax.all_gather(current, "cols", axis=1, tiled=True)
+        gathered = jnp.concatenate(
+            lax.all_to_all(jnp.stack([current] * lax.axis_size("cols")), "cols", 0, 0), axis=1
+        )
         all_blocks = gathered.reshape(rows_here, nblocks_all, block_size)
         selected = jnp.take(all_blocks, pattern[layer].reshape(-1), axis=1)
         items = selected.shape[0]

time: 416 us -> 888 us (2.13)
  waiting for transfers between devices: 296 us -> 719 us
  starting transfers between devices: 0.31 us -> 33.1 us
  local copies, waits for them, and re-layouts: 81.9 us -> 93.1 us
    all_to_all x0 -> x2, waiting for transfers between devices: none -> 718 us  [per_device(): lax.all_to_all(jnp.stack([current] * lax.axis_size('cols')), 'cols', 0, 0)]
    all_gather x2 -> x0, waiting for transfers between devices: 295 us -> none  [per_device(): gathered = lax.all_gather(current, 'cols', axis=1, tiled=True)]
    another operation x0 -> x4, local copies, waits for them, and re-layouts: none -> 57.6 us  [the longest x2 44.8 us: per_device(): all_blocks = gathered.reshape(rows_here, nblocks_all, block_size)]
    reshape x2, local copies, waits for them, and re-layouts: 45.3 us -> 0.27 us  [per_device(): shifted = total.reshape(items, owned * block_size) + layer_bias[None, :]]
    all_to_all x0 -> x2, starting transfers between devices: none -> 32.9 us  [per_device(): lax.all_to_all(jnp.stack([current] * lax.axis_size('cols')), 'cols', 0, 0)]
  transfers between devices with their start and end apart: 4 -> 4, of which waited for: 2 -> 2; matrix products, arithmetic and copies ran while one was open for 22% -> 10% of each run, Pallas kernels for 0% -> 0%
where the time goes in v1:
time: 888 us; the launch traced here: 882 us
  waiting for transfers between devices  719 us (81%)
  local copies, waits for them, and re-layouts  93.1 us (10%)
  starting transfers between devices  33.1 us (4%)
  between operations  13.6 us (2%)
  matrix products  12.2 us (1%)
  other arithmetic  11.6 us (1%)
    all_to_all x2, waiting for transfers between devices, per_device(): lax.all_to_all(jnp.stack([current] * lax.axis_size('cols')), 'cols', 0, 0)  718 us
    another operation x2, local copies, waits for them, and re-layouts, per_device(): all_blocks = gathered.reshape(rows_here, nblocks_all, block_size)  44.8 us
    all_to_all x2, starting transfers between devices, per_device(): lax.all_to_all(jnp.stack([current] * lax.axis_size('cols')), 'cols', 0, 0)  32.9 us
    gather x2, local copies, waits for them, and re-layouts, per_device(): selected = jnp.take(all_blocks, pattern[layer].reshape(-1), axis=1)  26.9 us
  transfers between devices with their start and end apart: 4, of which 2 were waited for; matrix products, arithmetic and copies ran while one was open for 10% of the time, Pallas kernels for 0%

profile of v1, /device:TPU:8, one launch (start us, length us, event | category | flops | bytes accessed | tf_op | source)
XLA Modules:
  0.0 882.4 jit_solution(1788812277605908067)
XLA Ops:
  6.5 1.0 copy.10
  7.6 6.4 stack.4
  14.0 15.8 %all-to-all-start = ((bf16[128,128,512]{1,2,0:T(8,128)(2,1)}), bf16[128,128,512]{1,2,0:T(8,128)(2,1)}, u32[]{:S(2)}, u32[]{:S(2)}) async-start(bf16[128,128,512]{1,2,0:T(8,128)(2,1)} %stack.4), calls=%async_computation | async-start | bytes 33554432 | tf_op jit(solution)/shard_map/all_to_all | solution.py:22
  29.8 0.0 copy-start
  29.8 0.0 copy-start.2
  29.8 0.0 copy-start.1
  29.8 0.0 all-gather.7.cloned.1.call-start
  29.9 7.0 fusion.6
  36.8 0.0 all-gather.7.cloned.1.call-update
  36.9 0.0 copy-done
  36.9 0.1 reshape_squeeze.6
  37.0 0.1 fusion.5
  37.1 356.0 %all-to-all-done = bf16[128,128,512]{1,2,0:T(8,128)(2,1)} async-done(((bf16[128,128,512]{1,2,0:T(8,128)(2,1)}), bf16[128,128,512]{1,2,0:T(8,128)(2,1)}, u32[]{:S(2)}, u32[]{:S(2)}) %all-to-all-start) | async-done | bytes 16777248 | tf_op jit(solution)/shard_map/all_to_all | solution.py:22
  393.1 22.4 %copy.11 = bf16[128,512,128]{2,0,1:T(8,128)(2,1)} copy(bf16[128,512,128]{0,2,1:T(8,128)(2,1)} %bitcast.5) | data formatting | bytes 33554432 | tf_op jit(solution)/shard_map/reshape;reshape | solution.py:24
  415.5 13.5 %gather_fusion = bf16[160,128,128]{2,1,0:T(8,128)(2,1)} fusion(bf16[128,512,128]{2,0,1:T(8,128)(2,1)} %copy.11, s32[1024]{0:T(1024)S(1)} %pad_clamp_fusion.1), kind=kCustom, calls=%fused_computation.clone | custom fusion | bytes 10486400 | tf_op jit(solution)/shard_map/jit(_take)/gather | solution.py:25
  429.0 5.3 broadcast_select_fusion.1
  434.3 6.1 fusion
  440.4 0.1 copy.13
  440.6 0.1 copy.14
  440.7 6.4 stack.5
  447.1 17.1 %all-to-all-start.1 = ((bf16[128,128,512]{1,2,0:T(8,128)(2,1)}), bf16[128,128,512]{1,2,0:T(8,128)(2,1)}, u32[]{:S(2)}, u32[]{:S(2)}) async-start(bf16[128,128,512]{1,2,0:T(8,128)(2,1)} %stack.5), calls=%async_computation.1 | async-start | bytes 33554432 | tf_op jit(solution)/shard_map/all_to_all | solution.py:22
  464.2 0.2 all-gather.5.cloned.1.call-start
  464.4 0.5 all-gather.5.cloned.1.call-update
  464.9 0.1 reshape_squeeze.7
  465.0 0.1 fusion.4
  465.1 362.3 %all-to-all-done.1 = bf16[128,128,512]{1,2,0:T(8,128)(2,1)} async-done(((bf16[128,128,512]{1,2,0:T(8,128)(2,1)}), bf16[128,128,512]{1,2,0:T(8,128)(2,1)}, u32[]{:S(2)}, u32[]{:S(2)}) %all-to-all-start.1) | async-done | bytes 16777248 | tf_op jit(solution)/shard_map/all_to_all | solution.py:22
  827.4 22.4 %copy.15 = bf16[128,512,128]{2,0,1:T(8,128)(2,1)} copy(bf16[128,512,128]{0,2,1:T(8,128)(2,1)} %bitcast.14) | data formatting | bytes 33554432 | tf_op jit(solution)/shard_map/reshape;reshape | solution.py:24
  849.8 13.5 %gather_fusion.1 = bf16[160,128,128]{2,1,0:T(8,128)(2,1)} fusion(bf16[128,512,128]{2,0,1:T(8,128)(2,1)} %copy.15, s32[1024]{0:T(1024)S(1)} %pad_clamp_fusion), kind=kCustom, calls=%fused_computation.1.clone | custom fusion | bytes 10486400 | tf_op jit(solution)/shard_map/jit(_take)/gather | solution.py:25
  863.3 5.3 broadcast_select_fusion
  868.6 6.1 fusion.1
  874.7 0.1 copy.17
  874.9 0.7 clamp_convert_fusion
  (14 shorter events, 0.1 us)
Async XLA Ops:
  14.0 379.1 %all-to-all-start = ((bf16[128,128,512]{1,2,0:T(8,128)(2,1)}), bf16[128,128,512]{1,2,0:T(8,128)(2,1)}, u32[]{:S(2)}, u32[]{:S(2)}) async-start(bf16[128,128,512]{1,2,0:T(8,128)(2,1)} %stack.4), calls=%async_computation | async-start | bytes 33554432 | tf_op jit(solution)/shard_map/all_to_all | solution.py:22
  29.8 7.1 copy-start
  29.8 7.2 copy-start.2
  29.8 7.3 copy-start.1
  29.8 404.5 %all-gather.7.cloned.1.call-start = ((), (), s32[]{:S(2)}) async-start(), calls=%async_computation.3 | async-start | bytes 7864320 | tf_op jit(solution)/shard_map/all_gather | solution.py:17
  447.1 380.3 %all-to-all-start.1 = ((bf16[128,128,512]{1,2,0:T(8,128)(2,1)}), bf16[128,128,512]{1,2,0:T(8,128)(2,1)}, u32[]{:S(2)}, u32[]{:S(2)}) async-start(bf16[128,128,512]{1,2,0:T(8,128)(2,1)} %stack.5), calls=%async_computation.1 | async-start | bytes 33554432 | tf_op jit(solution)/shard_map/all_to_all | solution.py:22
  464.2 404.5 %all-gather.5.cloned.1.call-start = ((), (), s32[]{:S(2)}) async-start(), calls=%async_computation.2 | async-start | bytes 7864320 | tf_op jit(solution)/shard_map/all_gather | solution.py:17
Sparse Core Ops, SparseCore 0:
  37.0 21.8 all-gather.6
  466.8 21.8 all-gather.4
